TPU v7x, 512 devices: a whole 4x8x8 slice. The times are simulated.
512 devices in a mesh: chan: 8 (over z), space: 64 (over y, x, core).
Axes of the slice: x: 4, y: 8, z: 8, core: 2. Of those that a mesh axis runs over, the one named last changes fastest.
Arguments:
- cotangent: bfloat16 [80, 131072], P(None, 'space'), may hold values from -6 to 6
- pair_band: int32 [8192], P('space'), may hold values from 0 to 15
- pair_target: int32 [8192], P('space'), may hold values from 0 to 1023, as said below
- pair_count: int32 [64], P('space'), may hold values from 1 to 128, as said below
- pair_weight: bfloat16 [8192, 128, 128], P('space'), may hold values from -0.5 to 0.5
- head_weight: bfloat16 [512, 80], P('chan'), may hold values from -0.25 to 0.25
- features: bfloat16 [512, 131072], P('chan', 'space'), may hold values from -6 to 6
Outputs:
- feature_grad: bfloat16 [512, 131072], P('chan', 'space')
- weight_grad: float32 [512, 80], P('chan')
Inputs may be any that keep to these rules, and one draw needn't show every extreme that they name: `pair_target`: targets of the slots of one device fall on each device's blocks (device index = target // 16) exactly 2 times, so at most 2 live pairs go from one device to one device; the first and last device of space have all slots live. `pair_count`: devices near both ends of space carry more live pairs than those in the middle.
All inputs are finite; a program needn't handle non-finite values.
Results may differ from a plain program's by a relative error of at most 0.0058.
Values may be sent and summed in bfloat16 or wider, within the bound.
No kernel may reach another device: no remote copies, remote signals or barrier semaphores. Data moves between devices by JAX's collectives and lax.ppermute only.
A program may use at most 64 MiB of HBM per device.

v0:
```python
import jax
import jax.numpy as jnp
from jax import lax
from jax.sharding import PartitionSpec as P


def on_device(cotangent, pair_band, pair_target, pair_count, pair_weight, head_weight, features):
    nspace = lax.axis_size("space")
    vars_all = cotangent.shape[0]
    ll_local = cotangent.shape[1]
    block_size = pair_weight.shape[1]
    pair_slots = pair_band.shape[0]
    hp_local = features.shape[1]
    hp_blocks = hp_local // block_size
    per_peer = pair_slots // nspace
    band_blocks = cotangent.reshape(vars_all, ll_local // block_size, block_size).transpose(1, 0, 2)
    picked = band_blocks[pair_band]
    contrib = jnp.einsum(
        "pvr,prq->pvq", picked, pair_weight, preferred_element_type=jnp.float32
    ).astype(jnp.bfloat16)
    pair_index = jnp.arange(pair_slots)
    live_pair = pair_index < pair_count[0]
    dest_device = pair_target // hp_blocks
    local_block = pair_target % hp_blocks
    earlier = (
        (dest_device[:, None] == dest_device[None, :])
        & live_pair[None, :]
        & (pair_index[None, :] < pair_index[:, None])
    )
    slot_rank = jnp.sum(earlier.astype(jnp.int32), axis=1)
    slot_index = jnp.where(live_pair, dest_device * per_peer + slot_rank, pair_slots)
    sendbuf = (
        jnp.zeros((pair_slots, vars_all, block_size), jnp.bfloat16)
        .at[slot_index]
        .set(contrib, mode="drop")
    )
    labels = (
        jnp.full((pair_slots,), -1.0, jnp.bfloat16)
        .at[slot_index]
        .set(local_block.astype(jnp.bfloat16), mode="drop")
    )
    sendbuf = sendbuf.reshape(nspace, per_peer, vars_all, block_size)
    labels = labels.reshape(nspace, per_peer)
    received, received_tags = (
        lax.all_to_all(sendbuf, "space", split_axis=0, concat_axis=0, tiled=True),
        lax.all_to_all(labels, "space", split_axis=0, concat_axis=0, tiled=True),
    )
    block_ids = jnp.arange(hp_blocks).astype(jnp.bfloat16)
    onehot = (received_tags.reshape(pair_slots)[:, None] == block_ids[None, :]).astype(jnp.bfloat16)
    summed = jnp.einsum(
        "sh,svq->vhq",
        onehot,
        received.reshape(pair_slots, vars_all, block_size),
        preferred_element_type=jnp.float32,
    )
    pixel_part = summed.astype(jnp.bfloat16).reshape(vars_all, hp_local)
    feature_grad = jnp.dot(head_weight, pixel_part, preferred_element_type=jnp.float32).astype(
        jnp.bfloat16
    )
    partial_value = lax.dot_general(
        features, pixel_part, (((1,), (1,)), ((), ())), preferred_element_type=jnp.float32
    )
    grad_scale = float(hp_local * nspace) ** (-0.5)
    weight_grad = lax.psum(partial_value, "space") * grad_scale
    return (feature_grad, weight_grad)


def solution(mesh):
    placed = (
        P(None, "space"),
        P("space"),
        P("space"),
        P("space"),
        P("space", None, None),
        P("chan", None),
        P("chan", "space"),
    )
    return jax.shard_map(
        on_device,
        mesh=mesh,
        in_specs=placed,
        out_specs=(P("chan", "space"), P("chan", None)),
        check_vma=False,
    )
```

profile of v0, /device:TPU:256, one launch (start us, length us, event | category | flops | bytes accessed | tf_op | source)
XLA Modules:
  0.0 362.7 jit_solution(4748789527923973483)
XLA Ops:
  0.6 0.0 copy-start
  0.6 0.7 fusion.10
  2.0 0.2 convert_reduce_fusion
  2.2 1.3 scatter_custom_fusion.1
  3.6 0.8 all_to_all.12
  4.4 10.6 %all-to-all-start.1 = ((bf16[64,1,2]{2,1,0:T(2,128)(2,1)}), bf16[64,1,2]{2,1,0:T(2,128)(2,1)S(1)}, u32[]{:S(2)}, u32[]{:S(2)}) async-start(bf16[64,1,2]{2,1,0:T(2,128)(2,1)} %all_to_all.12), calls=%async_computation.1 | async-start | bytes 65536 | tf_op jit(solution)/shard_map/all_to_all | solution.py:46
  14.9 0.0 copy-done
  14.9 0.1 bitcast_bitcast_fusion
  15.0 0.7 compare_select_fusion
  15.7 1.1 gather_fusion
  16.7 5.2 %convolution_convert_fusion.1 = bf16[128,80,128]{2,1,0:T(8,128)(2,1)} fusion(bf16[128,80,128]{2,1,0:T(8,128)(2,1)S(1)} %gather_fusion, bf16[128,128,128]{2,1,0:T(8,128)(2,1)} %param.11), kind=kOutput, calls=%fused_computation.5 | convolution fusion | flops 336855040 | bytes 9437184 | tf_op jit(solution)/shard_map/pvr,prq->pvq/dot_general | solution.py:18
  22.0 0.3 broadcast_in_dim.12
  22.3 12.1 %scatter_fusion = bf16[128,80,128]{2,1,0:T(8,128)(2,1)S(1)} fusion(bf16[128,80,128]{2,1,0:T(8,128)(2,1)S(1)} %broadcast_in_dim.12, s32[128]{0:T(128)S(1)} %compare_select_fusion.1, bf16[128,80,128]{2,1,0:T(8,128)(2,1)} %convolution_convert_fusion.1), kind=kCustom, calls=%fused_computation.1 | custom fusion | bytes 7864832 | tf_op jit(solution)/shard_map/scatter | solution.py:35
  34.5 3.6 copy.17
  38.0 0.0 all-to-all-done.1
  38.0 10.5 %all-to-all-start = ((bf16[64,2,80,128]{3,1,2,0:T(2,128)(2,1)}), bf16[64,2,80,128]{3,1,2,0:T(2,128)(2,1)S(1)}, u32[]{:S(2)}, u32[]{:S(2)}) async-start(bf16[64,2,80,128]{3,1,2,0:T(2,128)(2,1)} %copy.17), calls=%async_computation | async-start | bytes 5242880 | tf_op jit(solution)/shard_map/all_to_all | solution.py:45
  48.5 0.1 reduce
  48.6 0.1 eq.33
  48.8 62.3 %all-to-all-done = bf16[64,2,80,128]{3,1,2,0:T(2,128)(2,1)S(1)} async-done(((bf16[64,2,80,128]{3,1,2,0:T(2,128)(2,1)}), bf16[64,2,80,128]{3,1,2,0:T(2,128)(2,1)S(1)}, u32[]{:S(2)}, u32[]{:S(2)}) %all-to-all-start) | async-done | bytes 2621472 | tf_op jit(solution)/shard_map/all_to_all | solution.py:45
  111.1 2.9 copy.18
  114.0 0.0 copy-start.1
  114.0 0.0 copy-start.2
  114.0 0.5 convolution_convert_fusion.2
  114.6 0.2 copy-done.1
  114.7 0.9 fusion
  115.7 0.0 copy-done.2
  115.7 0.2 convolution_bitcast_fusion
  115.9 246.1 %psum.7 = f32[64,80]{1,0:T(8,128)S(1)} all-reduce(f32[64,80]{1,0:T(8,128)S(1)} %convolution_bitcast_fusion), channel_id=1, replica_groups=mesh['chan'=8,'space'=64] {'space'}, use_global_device_ids=true, to_apply=%region_3.4 | all-reduce | flops 5120 | bytes 40960 | tf_op jit(solution)/shard_map/psum | solution.py:64
  362.1 0.6 broadcast_multiply_fusion
  (4 shorter events, 0.0 us)
Async XLA Ops:
  0.6 14.3 %copy-start = (bf16[80,2048]{1,0:T(8,128)(2,1)S(1)}, bf16[80,2048]{1,0:T(8,128)(2,1)}, u32[]{:S(2)}) copy-start(bf16[80,2048]{1,0:T(8,128)(2,1)} %param.7) | copy-start | bytes 983044
  4.4 33.7 %all-to-all-start.1 = ((bf16[64,1,2]{2,1,0:T(2,128)(2,1)}), bf16[64,1,2]{2,1,0:T(2,128)(2,1)S(1)}, u32[]{:S(2)}, u32[]{:S(2)}) async-start(bf16[64,1,2]{2,1,0:T(2,128)(2,1)} %all_to_all.12), calls=%async_computation.1 | async-start | bytes 65536 | tf_op jit(solution)/shard_map/all_to_all | solution.py:46
  38.0 73.1 %all-to-all-start = ((bf16[64,2,80,128]{3,1,2,0:T(2,128)(2,1)}), bf16[64,2,80,128]{3,1,2,0:T(2,128)(2,1)S(1)}, u32[]{:S(2)}, u32[]{:S(2)}) async-start(bf16[64,2,80,128]{3,1,2,0:T(2,128)(2,1)} %copy.17), calls=%async_computation | async-start | bytes 5242880 | tf_op jit(solution)/shard_map/all_to_all | solution.py:45
  114.0 0.7 copy-start.1
  114.0 1.6 copy-start.2
where the time goes:
time: 363 us
  blocking collectives  246 us (68%)
  waiting for transfers between devices  62.4 us (17%)
  local copies, waits for them, and re-layouts  22.6 us (6%)
  starting transfers between devices  21 us (6%)
  matrix products  6.89 us (2%)
    psum x1, blocking collectives, on_device(): weight_grad = lax.psum(partial_value, 'space') * grad_scale  246 us
    all_to_all x1, waiting for transfers between devices, on_device(): lax.all_to_all(sendbuf, 'space', split_axis=0, concat_axis=0, tiled=True)  62.3 us
    scatter x1, local copies, waits for them, and re-layouts, on_device(): sendbuf = jnp.zeros((pair_slots, vars_all, block_size), jnp.bfloat16).at[...  12.1 us
    all_to_all x1, starting transfers between devices, on_device(): lax.all_to_all(labels, 'space', split_axis=0, concat_axis=0, tiled=True)  10.6 us
    all_to_all x1, starting transfers between devices, on_device(): lax.all_to_all(sendbuf, 'space', split_axis=0, concat_axis=0, tiled=True)  10.5 us
  transfers between devices with their start and end apart: 2, of which 1 were waited for; matrix products, arithmetic and copies ran while one was open for 6% of the time, Pallas kernels for 0%

commit v1 on v0

--- a/solution.py
+++ b/solution.py
@@ -61,7 +61,7 @@
         features, pixel_part, (((1,), (1,)), ((), ())), preferred_element_type=jnp.float32
     )
     grad_scale = float(hp_local * nspace) ** (-0.5)
-    weight_grad = lax.psum(partial_value, "space") * grad_scale
+    weight_grad = jnp.sum(lax.all_gather(partial_value, "space"), axis=0) * grad_scale
     return (feature_grad, weight_grad)
 
 

time: 363 us -> 216 us (0.60)
  the two profiles are of different devices: /device:TPU:256 before, /device:TPU:1 now
where the time goes in v1:
time: 216 us; the launch traced here: 215 us
  waiting for transfers between devices  144 us (67%)
  local copies, waits for them, and re-layouts  22.8 us (11%)
  starting transfers between devices  22.1 us (10%)
  between operations  14.8 us (7%)
  matrix products  7.5 us (3%)
  other arithmetic  4.06 us (2%)
    all_gather x1, waiting for transfers between devices, on_device(): lax.all_gather(partial_value, 'space')  83.2 us
    all_to_all x1, waiting for transfers between devices, on_device(): lax.all_to_all(sendbuf, 'space', split_axis=0, concat_axis=0, tiled=True)  60.6 us
    scatter x1, local copies, waits for them, and re-layouts, on_device(): sendbuf = jnp.zeros((pair_slots, vars_all, block_size), jnp.bfloat16).at[...  12.2 us
    all_to_all x1, starting transfers between devices, on_device(): lax.all_to_all(labels, 'space', split_axis=0, concat_axis=0, tiled=True)  11.6 us
    all_to_all x1, starting transfers between devices, on_device(): lax.all_to_all(sendbuf, 'space', split_axis=0, concat_axis=0, tiled=True)  10.4 us
    dot_general x1, matrix products, on_device(): jnp.einsum('pvr,prq->pvq', picked, pair_weight, preferred_element_type=jn...  5.22 us
  transfers between devices with their start and end apart: 3, of which 2 were waited for; matrix products, arithmetic and copies ran while one was open for 11% of the time, Pallas kernels for 0%

profile of v1, /device:TPU:1, one launch (start us, length us, event | category | flops | bytes accessed | tf_op | source)
XLA Modules:
  0.0 215.0 jit_solution(2081098586910395095)
XLA Ops:
  7.2 0.0 copy-start
  7.2 0.7 fusion.10
  8.6 0.2 convert_reduce_fusion
  8.7 1.3 scatter_custom_fusion.1
  10.1 0.8 all_to_all.12
  10.9 11.6 %all-to-all-start.1 = ((bf16[64,1,2]{2,1,0:T(2,128)(2,1)}), bf16[64,1,2]{2,1,0:T(2,128)(2,1)S(1)}, u32[]{:S(2)}, u32[]{:S(2)}) async-start(bf16[64,1,2]{2,1,0:T(2,128)(2,1)} %all_to_all.12), calls=%async_computation.1 | async-start | bytes 65536 | tf_op jit(solution)/shard_map/all_to_all | solution.py:46
  22.5 0.0 copy-done
  22.5 0.1 bitcast_bitcast_fusion
  22.6 0.7 compare_select_fusion
  23.2 1.1 gather_fusion
  24.3 5.2 %convolution_convert_fusion.1 = bf16[128,80,128]{2,1,0:T(8,128)(2,1)} fusion(bf16[128,80,128]{2,1,0:T(8,128)(2,1)S(1)} %gather_fusion, bf16[128,128,128]{2,1,0:T(8,128)(2,1)} %param.11), kind=kOutput, calls=%fused_computation.5 | convolution fusion | flops 336855040 | bytes 9437184 | tf_op jit(solution)/shard_map/pvr,prq->pvq/dot_general | solution.py:18
  29.5 0.3 broadcast_in_dim.12
  29.9 12.2 %scatter_fusion = bf16[128,80,128]{2,1,0:T(8,128)(2,1)S(1)} fusion(bf16[128,80,128]{2,1,0:T(8,128)(2,1)S(1)} %broadcast_in_dim.12, s32[128]{0:T(128)S(1)} %compare_select_fusion.1, bf16[128,80,128]{2,1,0:T(8,128)(2,1)} %convolution_convert_fusion.1), kind=kCustom, calls=%fused_computation.1 | custom fusion | bytes 7864832 | tf_op jit(solution)/shard_map/scatter | solution.py:35
  42.0 3.6 %copy.17 = bf16[64,2,80,128]{3,1,2,0:T(2,128)(2,1)} copy(bf16[64,2,80,128]{3,2,1,0:T(8,128)(2,1)S(1)} %bitcast.32) | data formatting | bytes 5242880 | tf_op jit(solution)/shard_map/reshape | solution.py:42
  45.6 0.0 all-to-all-done.1
  45.6 10.4 %all-to-all-start = ((bf16[64,2,80,128]{3,1,2,0:T(2,128)(2,1)}), bf16[64,2,80,128]{3,1,2,0:T(2,128)(2,1)S(1)}, u32[]{:S(2)}, u32[]{:S(2)}) async-start(bf16[64,2,80,128]{3,1,2,0:T(2,128)(2,1)} %copy.17), calls=%async_computation | async-start | bytes 5242880 | tf_op jit(solution)/shard_map/all_to_all | solution.py:45
  56.1 0.0 all-gather.3.cloned.1.call-start
  56.1 0.1 reduce
  56.2 0.1 eq.33
  56.4 60.6 %all-to-all-done = bf16[64,2,80,128]{3,1,2,0:T(2,128)(2,1)S(1)} async-done(((bf16[64,2,80,128]{3,1,2,0:T(2,128)(2,1)}), bf16[64,2,80,128]{3,1,2,0:T(2,128)(2,1)S(1)}, u32[]{:S(2)}, u32[]{:S(2)}) %all-to-all-start) | async-done | bytes 2621472 | tf_op jit(solution)/shard_map/all_to_all | solution.py:45
  117.0 2.9 %copy.18 = bf16[64,2,80,128]{3,1,0,2:T(2,128)(2,1)S(1)} copy(bf16[64,2,80,128]{3,1,2,0:T(2,128)(2,1)S(1)} %all-to-all-done) | data formatting | bytes 5242880 | tf_op jit(solution)/shard_map/all_to_all | solution.py:45
  119.9 0.0 copy-start.2
  119.9 0.0 copy-start.1
  119.9 0.5 convolution_convert_fusion.2
  120.4 0.4 copy-done.2
  120.8 0.9 convolution_bitcast_fusion
  121.7 0.0 all-gather.3.cloned.1.call-update
  121.7 0.0 copy-done.1
  121.7 0.9 fusion
  122.6 83.2 %all-gather.3.cloned.1.call-done = f32[4096,80]{1,0:T(8,128)} async-done(((f32[64,80]{1,0:T(8,128)}), f32[4096,80]{1,0:T(8,128)}) %all-gather.3.cloned.1.call-update) | async-done | bytes 1310736 | tf_op jit(solution)/shard_map/all_gather | solution.py:64
  205.8 1.8 reduce_sum.19
  207.6 0.6 broadcast_multiply_fusion
  (4 shorter events, 0.0 us)
Async XLA Ops:
  7.2 15.3 %copy-start = (bf16[80,2048]{1,0:T(8,128)(2,1)S(1)}, bf16[80,2048]{1,0:T(8,128)(2,1)}, u32[]{:S(2)}) copy-start(bf16[80,2048]{1,0:T(8,128)(2,1)} %param.7) | copy-start | bytes 983044
  10.9 34.7 %all-to-all-start.1 = ((bf16[64,1,2]{2,1,0:T(2,128)(2,1)}), bf16[64,1,2]{2,1,0:T(2,128)(2,1)S(1)}, u32[]{:S(2)}, u32[]{:S(2)}) async-start(bf16[64,1,2]{2,1,0:T(2,128)(2,1)} %all_to_all.12), calls=%async_computation.1 | async-start | bytes 65536 | tf_op jit(solution)/shard_map/all_to_all | solution.py:46
  45.6 71.3 %all-to-all-start = ((bf16[64,2,80,128]{3,1,2,0:T(2,128)(2,1)}), bf16[64,2,80,128]{3,1,2,0:T(2,128)(2,1)S(1)}, u32[]{:S(2)}, u32[]{:S(2)}) async-start(bf16[64,2,80,128]{3,1,2,0:T(2,128)(2,1)} %copy.17), calls=%async_computation | async-start | bytes 5242880 | tf_op jit(solution)/shard_map/all_to_all | solution.py:45
  56.1 149.7 %all-gather.3.cloned.1.call-start = ((), (), s32[]{:S(2)}) async-start(), calls=%async_computation.2 | async-start | bytes 2129920 | tf_op jit(solution)/shard_map/all_gather | solution.py:64
  119.9 1.0 copy-start.2
  119.9 1.8 copy-start.1
Sparse Core Ops, SparseCore 0:
  121.8 83.9 all-gather.2
